TPU v7x, 256 devices: a whole 4x4x8 slice. The times are simulated.
256 devices in a mesh: space: 8 (over x, core), mem: 32 (over z, y).
Axes of the slice: x: 4, y: 4, z: 8, core: 2. Of those that a mesh axis runs over, the one named last changes fastest.
Arguments:
- prior_ensemble: float32 [512, 65536], P('mem', 'space'), may hold values from -5 to 5
- terminal_particles: float32 [512, 65536], P(None, ('space', 'mem')), may hold values from -5 to 5
- reverse_perturbation: float32 [3, 512, 65536], P(None, None, ('space', 'mem')), may hold values from -6 to 6
- measured_angles: float32 [65536], P(('space', 'mem')), may hold values from -1.3 to 1.3
Outputs:
- analysis: float32 [512, 65536], P(None, ('space', 'mem'))
All inputs are finite; a program needn't handle non-finite values.
Results may differ from a plain program's by a relative error of at most 0.0003.
Values sent between devices are 32-bit elements; how exact they have to be, the bound alone decides.
No kernel may reach another device: no remote copies, remote signals or barrier semaphores. Data moves between devices by JAX's collectives and lax.ppermute only.
A program may use at most 64 MiB of HBM per device.

v0:
```python
import math
import jax
import jax.numpy as jnp
from jax import lax
from jax.sharding import PartitionSpec as P

ITERS = 3


def member_weights(inner_pairing_matrix, particle_lengths, alpha, sigma2, temper):
    logits = (2.0 * alpha * inner_pairing_matrix - alpha * alpha * particle_lengths[None, :]) / (
        2.0 * sigma2 * temper
    )
    return jax.nn.softmax(logits, axis=1)


def per_device(prior_ensemble, terminal_particles, reverse_perturbation, measured_angles):
    peak_log_likelihood = lax.Precision.HIGHEST
    particle_vectors = lax.all_to_all(
        prior_ensemble, "mem", split_axis=1, concat_axis=0, tiled=True
    )
    devices_all = lax.axis_size("space") * lax.axis_size("mem")
    temper = math.sqrt(particle_vectors.shape[1] * devices_all)
    particle_lengths = lax.psum(
        jnp.sum(particle_vectors * particle_vectors, axis=1), ("space", "mem")
    )
    gaussian_variates = terminal_particles
    for step in range(ITERS):
        t = 1.0 - step / ITERS
        dt = 1.0 / ITERS
        alpha = 1.0 - 0.5 * t
        drift = -0.5 / alpha
        g2 = 1.0 + t / alpha
        damp = 1.0 - t
        partial_gram = jnp.einsum(
            "sv,mv->sm",
            gaussian_variates,
            particle_vectors,
            precision=peak_log_likelihood,
            preferred_element_type=jnp.float32,
        )
        inner_pairing_matrix = lax.psum(partial_gram, ("space", "mem"))
        annealed_importance = member_weights(
            inner_pairing_matrix, particle_lengths, alpha, t, temper
        )
        mixed_correction = jnp.dot(
            annealed_importance,
            particle_vectors,
            precision=peak_log_likelihood,
            preferred_element_type=jnp.float32,
        )
        score = -(gaussian_variates - alpha * mixed_correction) / t + damp * 4.0 * (
            measured_angles[None, :] - jnp.arctan(gaussian_variates)
        ) / (1.0 + gaussian_variates * gaussian_variates)
        gaussian_variates = (
            gaussian_variates
            + dt * (-drift * gaussian_variates + g2 * score)
            + math.sqrt(dt * g2) * reverse_perturbation[step]
        )
    return gaussian_variates


def solution(mesh):
    in_specs = (
        P("mem", "space"),
        P(None, ("space", "mem")),
        P(None, None, ("space", "mem")),
        P(("space", "mem")),
    )
    out_specs = P(None, ("space", "mem"))
    return jax.shard_map(
        per_device, mesh=mesh, in_specs=in_specs, out_specs=out_specs, check_vma=False
    )
```

profile of v0, /device:TPU:2, one launch (start us, length us, event | category | flops | bytes accessed | tf_op | source)
XLA Modules:
  0.0 836.8 jit_solution(16117803827665191883)
XLA Ops:
  6.5 0.0 all-reduce.4.cloned.1.call-start
  6.5 1.2 copy.9
  7.7 29.0 %all_to_all.19 = f32[16,32,256]{2,0,1:T(8,128)S(1)} all-to-all(f32[16,32,256]{2,0,1:T(8,128)S(1)} %bitcast.30), channel_id=1, replica_groups=mesh['space'=8,'mem'=32] {'mem'}, dimensions={1} | all-to-all | bytes 1048576 | tf_op jit(solution)/shard_map/all_to_all | solution.py:19
  36.7 0.0 copy-done.3
  36.7 2.1 fusion.2
  38.8 0.0 all-reduce.4.cloned.1.call-update
  38.8 0.0 all-reduce.6.cloned.1.call-start
  38.8 0.0 copy-done
  38.8 0.1 fusion
  39.0 0.1 reduce_sum.39
  39.1 72.9 %psum.29 = f32[512]{0:T(512)S(1)} all-reduce(f32[512]{0:T(512)S(1)} %reduce_sum.39), channel_id=1, replica_groups=mesh['space'=8,'mem'=32] {'space','mem'}, use_global_device_ids=true, to_apply=%region_2.0 | all-reduce | flops 512 | bytes 4096 | tf_op jit(solution)/shard_map/psum | solution.py:24
  112.0 179.0 %all-reduce.4.cloned.1.call-done = f32[512,512]{1,0:T(8,128)} async-done(((f32[512,512]{1,0:T(8,128)}), f32[512,512]{1,0:T(8,128)}) %all-reduce.4.cloned.1.call-update) | async-done | bytes 1048592 | tf_op jit(solution)/shard_map/psum | solution.py:42
  291.0 2.4 subtract_multiply_fusion.2
  293.4 3.7 online-softmax
  297.1 0.0 copy-done.6
  297.1 0.0 copy-done.1
  297.1 0.0 copy-done.5
  297.1 3.9 fusion.1
  301.1 0.0 all-reduce.6.cloned.1.call-update
  301.1 0.2 all-reduce.8.cloned.1.call-start
  301.3 254.5 %all-reduce.6.cloned.1.call-done = f32[512,512]{1,0:T(8,128)} async-done(((f32[512,512]{1,0:T(8,128)}), f32[512,512]{1,0:T(8,128)}) %all-reduce.6.cloned.1.call-update) | async-done | bytes 1048592 | tf_op jit(solution)/shard_map/psum | solution.py:42
  555.8 2.4 subtract_multiply_fusion.1
  558.2 3.6 online-softmax.1
  561.8 0.0 copy-done.4
  561.8 2.8 bitcast_add_fusion.1
  564.6 0.0 copy-done.2
  564.6 2.1 fusion.3
  566.7 0.0 all-reduce.8.cloned.1.call-update
  566.7 254.9 %all-reduce.8.cloned.1.call-done = f32[512,512]{1,0:T(8,128)} async-done(((f32[512,512]{1,0:T(8,128)}), f32[512,512]{1,0:T(8,128)}) %all-reduce.8.cloned.1.call-update) | async-done | bytes 1048592 | tf_op jit(solution)/shard_map/psum | solution.py:42
  821.6 2.4 subtract_multiply_fusion
  824.0 3.6 online-softmax.2
  827.6 2.7 bitcast_add_fusion
  (8 shorter events, 0.0 us)
Async XLA Ops:
  6.5 30.2 %copy-start.3 = (f32[512,256]{1,0:T(8,128)S(1)}, f32[512,256]{1,0:T(8,128)}, u32[]{:S(2)}) copy-start(f32[512,256]{1,0:T(8,128)} %param.5) | copy-start | bytes 1572868
  6.5 284.5 %all-reduce.4.cloned.1.call-start = ((), (), s32[]{:S(2)}) async-start(), calls=%async_computation.1 | async-start | bytes 2097152 | tf_op jit(solution)/shard_map/psum | solution.py:42
  36.7 2.1 copy-start
  38.8 517.0 %all-reduce.6.cloned.1.call-start = ((), (), s32[]{:S(2)}) async-start(), calls=%async_computation.2 | async-start | bytes 2097152 | tf_op jit(solution)/shard_map/psum | solution.py:42
  291.0 6.1 copy-start.6
  293.4 3.7 copy-start.1
  293.4 3.7 copy-start.5
  301.1 520.5 %all-reduce.8.cloned.1.call-start = ((), (), s32[]{:S(2)}) async-start(), calls=%async_computation.3 | async-start | bytes 2097152 | tf_op jit(solution)/shard_map/psum | solution.py:42
  558.2 3.6 copy-start.4
  561.8 2.8 copy-start.2
Sparse Core Ops, SparseCore 0:
  38.9 252.0 all-reduce.3
  301.2 254.5 all-reduce.5
  566.8 254.7 all-reduce.7
where the time goes:
time: 837 us
  waiting for transfers between devices  688 us (82%)
  blocking collectives  102 us (12%)
  between operations  13.1 us (2%)
  other arithmetic  12.8 us (2%)
  Pallas kernels  10.9 us (1%)
    psum x3, waiting for transfers between devices, per_device(): inner_pairing_matrix = lax.psum(partial_gram, ('space', 'mem'))  688 us
    psum x1, blocking collectives, per_device(): lax.psum(jnp.sum(particle_vectors * particle_vectors, axis=1), ('space',...  72.9 us
    all_to_all x1, blocking collectives, per_device(): lax.all_to_all(prior_ensemble, 'mem', split_axis=1, concat_axis=0, tiled=...  29 us
  transfers between devices with their start and end apart: 3, of which 3 were waited for; matrix products, arithmetic and copies ran while one was open for 0% of the time, Pallas kernels for 0%

commit v1 on v0

--- a/solution.py
+++ b/solution.py
@@ -39,7 +39,7 @@
             precision=peak_log_likelihood,
             preferred_element_type=jnp.float32,
         )
-        inner_pairing_matrix = lax.psum(partial_gram, ("space", "mem"))
+        inner_pairing_matrix = lax.psum(lax.psum(partial_gram, "mem"), "space")
         annealed_importance = member_weights(
             inner_pairing_matrix, particle_lengths, alpha, t, temper
         )

time: 837 us -> 725 us (0.87)
  waiting for transfers between devices: 688 us -> 573 us
    psum x3 -> x6, waiting for transfers between devices: 688 us -> 573 us  [per_device(): inner_pairing_matrix = lax.psum(lax.psum(partial_gram, 'mem'), 'space')]
  transfers between devices with their start and end apart: 3 -> 6, of which waited for: 3 -> 5; matrix products, arithmetic and copies ran while one was open for 0% -> 0% of each run, Pallas kernels for 0% -> 0%
where the time goes in v1:
time: 725 us; the launch traced here: 722 us
  waiting for transfers between devices  573 us (79%)
  blocking collectives  102 us (14%)
  between operations  13.5 us (2%)
  other arithmetic  12.7 us (2%)
  Pallas kernels  10.9 us (2%)
  matrix products  8.04 us (1%)
    psum x6, waiting for transfers between devices, per_device(): inner_pairing_matrix = lax.psum(lax.psum(partial_gram, 'mem'), 'space')  573 us
    psum x1, blocking collectives, per_device(): lax.psum(jnp.sum(particle_vectors * particle_vectors, axis=1), ('space',...  73 us
    all_to_all x1, blocking collectives, per_device(): lax.all_to_all(prior_ensemble, 'mem', split_axis=1, concat_axis=0, tiled=...  29 us
  transfers between devices with their start and end apart: 6, of which 5 were waited for; matrix products, arithmetic and copies ran while one was open for 0% of the time, Pallas kernels for 0%

profile of v1, /device:TPU:2, one launch (start us, length us, event | category | flops | bytes accessed | tf_op | source)
XLA Modules:
  0.0 721.9 jit_solution(6922162133194333580)
XLA Ops:
  6.5 1.2 copy.9
  7.7 29.0 %all_to_all.19 = f32[16,32,256]{2,0,1:T(8,128)S(1)} all-to-all(f32[16,32,256]{2,0,1:T(8,128)S(1)} %bitcast.30), channel_id=1, replica_groups=mesh['space'=8,'mem'=32] {'mem'}, dimensions={1} | all-to-all | bytes 1048576 | tf_op jit(solution)/shard_map/all_to_all | solution.py:19
  36.7 2.1 fusion.2
  38.8 0.0 all-reduce.7.cloned.1.call-update
  38.8 0.0 all-reduce.9.cloned.1.call-start
  38.8 145.9 %all-reduce.7.cloned.1.call-done = f32[512,512]{1,0:T(8,128)} async-done(((f32[512,512]{1,0:T(8,128)}), f32[512,512]{1,0:T(8,128)}) %all-reduce.7.cloned.1.call-update) | async-done | bytes 1048592 | tf_op jit(solution)/shard_map/psum | solution.py:42
  184.7 0.0 all-reduce.9.cloned.1.call-update
  184.7 0.0 all-reduce.11.cloned.1.call-start
  184.8 0.1 fusion
  184.9 0.1 reduce_sum.39
  185.0 73.0 %psum.51 = f32[512]{0:T(512)S(1)} all-reduce(f32[512]{0:T(512)S(1)} %reduce_sum.39), channel_id=1, replica_groups=mesh['space'=8,'mem'=32] {'space','mem'}, use_global_device_ids=true, to_apply=%region_3.0 | all-reduce | flops 512 | bytes 4096 | tf_op jit(solution)/shard_map/psum | solution.py:24
  258.0 2.3 subtract_multiply_fusion.2
  260.3 3.7 online-softmax
  264.1 3.9 fusion.1
  268.0 0.0 all-reduce.11.cloned.1.call-update
  268.0 0.0 all-reduce.13.cloned.1.call-start
  268.0 146.6 %all-reduce.11.cloned.1.call-done = f32[512,512]{1,0:T(8,128)} async-done(((f32[512,512]{1,0:T(8,128)}), f32[512,512]{1,0:T(8,128)}) %all-reduce.11.cloned.1.call-update) | async-done | bytes 1048592 | tf_op jit(solution)/shard_map/psum | solution.py:42
  414.6 0.0 all-reduce.13.cloned.1.call-update
  414.7 0.0 all-reduce.15.cloned.1.call-start
  414.7 64.7 %all-reduce.13.cloned.1.call-done = f32[512,512]{1,0:T(8,128)} async-done(((f32[512,512]{1,0:T(8,128)}), f32[512,512]{1,0:T(8,128)}) %all-reduce.13.cloned.1.call-update) | async-done | bytes 1048592 | tf_op jit(solution)/shard_map/psum | solution.py:42
  479.5 2.3 subtract_multiply_fusion.1
  481.8 3.6 online-softmax.1
  485.4 2.8 bitcast_add_fusion.1
  488.2 2.1 fusion.3
  490.3 0.0 all-reduce.15.cloned.1.call-update
  490.3 0.2 all-reduce.17.cloned.1.call-start
  490.5 151.1 %all-reduce.15.cloned.1.call-done = f32[512,512]{1,0:T(8,128)} async-done(((f32[512,512]{1,0:T(8,128)}), f32[512,512]{1,0:T(8,128)}) %all-reduce.15.cloned.1.call-update) | async-done | bytes 1048592 | tf_op jit(solution)/shard_map/psum | solution.py:42
  641.6 0.0 all-reduce.17.cloned.1.call-update
  641.6 64.8 %all-reduce.17.cloned.1.call-done = f32[512,512]{1,0:T(8,128)} async-done(((f32[512,512]{1,0:T(8,128)}), f32[512,512]{1,0:T(8,128)}) %all-reduce.17.cloned.1.call-update) | async-done | bytes 1048592 | tf_op jit(solution)/shard_map/psum | solution.py:42
  706.4 2.3 subtract_multiply_fusion
  708.8 3.6 online-softmax.2
  712.4 2.7 bitcast_add_fusion
  (17 shorter events, 0.0 us)
Async XLA Ops:
  6.5 30.2 %copy-start.3 = (f32[512,256]{1,0:T(8,128)S(1)}, f32[512,256]{1,0:T(8,128)}, u32[]{:S(2)}) copy-start(f32[512,256]{1,0:T(8,128)} %param.5) | copy-start | bytes 1572868
  6.5 178.2 %all-reduce.7.cloned.1.call-start = ((), (), s32[]{:S(2)}) async-start(), calls=%async_computation.1 | async-start | bytes 2097152 | tf_op jit(solution)/shard_map/psum | solution.py:42
  36.7 148.1 %copy-start = (f32[16,32,256]{2,0,1:T(8,128)}, f32[16,32,256]{2,0,1:T(8,128)S(1)}, u32[]{:S(2)}) copy-start(f32[16,32,256]{2,0,1:T(8,128)S(1)} %all_to_all.19) | copy-start | bytes 1572868
  38.8 219.2 %all-reduce.9.cloned.1.call-start = ((), (), s32[]{:S(2)}) async-start(), calls=%async_computation.2 | async-start | bytes 2097152 | tf_op jit(solution)/shard_map/psum | solution.py:42
  184.7 229.9 %all-reduce.11.cloned.1.call-start = ((), (), s32[]{:S(2)}) async-start(), calls=%async_computation.3 | async-start | bytes 2097152 | tf_op jit(solution)/shard_map/psum | solution.py:42
  258.0 6.1 copy-start.6
  260.3 3.7 copy-start.1
  260.3 3.7 copy-start.5
  268.0 211.5 %all-reduce.13.cloned.1.call-start = ((), (), s32[]{:S(2)}) async-start(), calls=%async_computation.4 | async-start | bytes 2097152 | tf_op jit(solution)/shard_map/psum | solution.py:42
  414.7 227.0 %all-reduce.15.cloned.1.call-start = ((), (), s32[]{:S(2)}) async-start(), calls=%async_computation.5 | async-start | bytes 2097152 | tf_op jit(solution)/shard_map/psum | solution.py:42
  481.8 3.6 copy-start.4
  485.4 2.8 copy-start.2
  490.3 216.1 %all-reduce.17.cloned.1.call-start = ((), (), s32[]{:S(2)}) async-start(), calls=%async_computation.6 | async-start | bytes 2097152 | tf_op jit(solution)/shard_map/psum | solution.py:42
Sparse Core Ops, SparseCore 0:
  38.9 145.7 all-reduce.6
  187.1 62.5 all-reduce.8
  268.1 146.4 all-reduce.10
  416.8 62.5 all-reduce.12
  490.4 151.1 all-reduce.14
  643.8 62.5 all-reduce.16
